TPU v7x, 32 devices: a whole 2x2x4 slice. The times are simulated.
32 devices in a mesh: rep: 2 (over x), ctx: 8 (over z, y), tp: 2 (over core).
Axes of the slice: x: 2, y: 2, z: 4, core: 2. Of those that a mesh axis runs over, the one named last changes fastest.
Arguments:
- queries: bfloat16 [4096, 4096], P(('rep', 'ctx'), 'tp'), parts along dimension 0, may hold values from -8 to 8
- rotated_key_rows: bfloat16 [4096, 512], P(('rep', 'ctx'), 'tp'), parts along dimension 0, may hold values from -8 to 8
- ordered_value_rows: bfloat16 [4096, 512], P(('rep', 'ctx'), 'tp'), parts along dimension 0, may hold values from -6 to 6
- block_order: int32 [32], P('rep'), parts along dimension 0, may hold values from 0 to 15, each once
- live_blocks: int32 [32, 12], P('rep'), parts along dimension 0, may hold values from -1 to 15, as said below
Outputs:
- attended: bfloat16 [4096, 4096], P(('rep', 'ctx', 'tp')), parts along dimension 0
- log_norm: float32 [64, 2048], P(('rep', 'tp'), 'ctx'), parts along dimension 0
There are 2 independent parts, one for each index of `rep`. A program takes and returns all parts, laid end to end along the dimension named above; each array names one. Nothing has to cross between parts.
Inputs may be any that keep to these rules, and one draw needn't show every extreme that they name: `live_blocks`: row s names block s in its first slot, then distinct blocks before s, then -1 in every unused slot; row 15 fills all 12 slots.
All inputs are finite; a program needn't handle non-finite values.
Results may differ from a plain program's by a relative error of at most 0.008.
Values may be sent and summed in bfloat16 or wider, within the bound.
A program may use at most 128 MiB of HBM per device.

v0:
```python
import jax
import jax.numpy as jnp
from jax import lax
from jax.sharding import PartitionSpec as P

HEAD_SIZE = 128
BLOCK_TOKENS = 128
NEG_LARGE = -1e30


def body(queries, rotated_key_rows, ordered_value_rows, block_order, live_blocks):
    tok_rows = queries.shape[0]
    kv_local = rotated_key_rows.shape[1] // HEAD_SIZE
    heads_local = queries.shape[1] // HEAD_SIZE
    query_groups = heads_local // kv_local
    blocks_total = block_order.shape[0]
    blocks_here = tok_rows // BLOCK_TOKENS
    factor = HEAD_SIZE ** (-0.5)
    shard_index = lax.axis_index("ctx")
    block_ids = jnp.arange(blocks_total, dtype=jnp.int32)
    my_blocks = lax.dynamic_slice_in_dim(block_order, shard_index * blocks_here, blocks_here)
    my_lists = jnp.take(live_blocks, my_blocks, axis=0)
    live_table = jnp.any(my_lists[:, :, None] == block_ids[None, None, :], axis=1)
    within = jnp.arange(BLOCK_TOKENS, dtype=jnp.int32)
    causal_square = within[None, :] <= within[:, None]
    query_heads = queries.reshape(tok_rows, kv_local, query_groups, HEAD_SIZE)
    carried = tuple(
        (
            (
                jnp.full((kv_local, query_groups, BLOCK_TOKENS), NEG_LARGE, jnp.float32),
                jnp.zeros((kv_local, query_groups, BLOCK_TOKENS), jnp.float32),
                jnp.zeros((kv_local, query_groups, BLOCK_TOKENS, HEAD_SIZE), jnp.float32),
            )
            for block_local in range(blocks_here)
        )
    )
    key_piece = lax.all_gather(rotated_key_rows, "ctx", axis=0, tiled=True)
    value_piece = lax.all_gather(ordered_value_rows, "ctx", axis=0, tiled=True)
    key_blocks = key_piece.shape[0] // BLOCK_TOKENS

    def one_key_block(turn_index, states):
        offset = turn_index * BLOCK_TOKENS
        key_part = lax.dynamic_slice_in_dim(key_piece, offset, BLOCK_TOKENS).reshape(
            BLOCK_TOKENS, kv_local, HEAD_SIZE
        )
        value_part = lax.dynamic_slice_in_dim(value_piece, offset, BLOCK_TOKENS).reshape(
            BLOCK_TOKENS, kv_local, HEAD_SIZE
        )
        key_seq = block_order[offset // BLOCK_TOKENS]
        updated = []
        for block_local in range(blocks_here):
            query_part = query_heads[block_local * BLOCK_TOKENS : (block_local + 1) * BLOCK_TOKENS]
            allowed = (key_seq != my_blocks[block_local]) | causal_square

            def compute_tile(current):
                running, denominator, weighted = current
                scores = (
                    jnp.einsum(
                        "qhgd,khd->hgqk", query_part, key_part, preferred_element_type=jnp.float32
                    )
                    * factor
                )
                scores = jnp.where(allowed, scores, NEG_LARGE)
                new_peak = jnp.maximum(running, jnp.max(scores, axis=-1))
                weights = jnp.where(allowed, jnp.exp(scores - new_peak[..., None]), 0.0)
                rescale = jnp.exp(running - new_peak)
                denominator = denominator * rescale + jnp.sum(weights, axis=-1)
                weighted = weighted * rescale[..., None] + jnp.einsum(
                    "hgqk,khd->hgqd",
                    weights.astype(jnp.bfloat16),
                    value_part,
                    preferred_element_type=jnp.float32,
                )
                return (new_peak, denominator, weighted)

            updated.append(
                lax.cond(
                    live_table[block_local, key_seq],
                    compute_tile,
                    lambda current: current,
                    states[block_local],
                )
            )
        return tuple(updated)

    states = lax.fori_loop(0, key_blocks, one_key_block, carried)
    running = jnp.concatenate([item[0] for item in states], axis=2)
    denominator = jnp.concatenate([item[1] for item in states], axis=2)
    weighted = jnp.concatenate([item[2] for item in states], axis=2)
    normed = weighted / denominator[..., None]
    merged_out = (
        jnp.transpose(normed, (2, 0, 1, 3))
        .reshape(tok_rows, heads_local * HEAD_SIZE)
        .astype(jnp.bfloat16)
    )
    log_norm = (running + jnp.log(denominator)).reshape(heads_local, tok_rows)
    attended = lax.all_to_all(merged_out, "tp", split_axis=0, concat_axis=1, tiled=True)
    return (attended, log_norm)


def solution(mesh):
    placed = (
        P(("rep", "ctx"), "tp"),
        P(("rep", "ctx"), "tp"),
        P(("rep", "ctx"), "tp"),
        P("rep"),
        P("rep", None),
    )
    return jax.shard_map(
        body,
        mesh=mesh,
        in_specs=placed,
        out_specs=(P(("rep", "ctx", "tp"), None), P(("rep", "tp"), "ctx")),
        check_vma=False,
    )
```

profile of v0, /device:TPU:0, one launch (start us, length us, event | category | flops | bytes accessed | tf_op | source)
XLA Modules:
  0.0 250.6 jit_solution(15988656583783142846)
XLA Ops:
  13.7 39.1 %all-gather.3.cloned.1.call-done = bf16[2048,256]{0,1:T(8,128)(2,1)} async-done(((bf16[256,256]{0,1:T(8,128)(2,1)}), bf16[2048,256]{0,1:T(8,128)(2,1)}) %all-gather.3.cloned.1.call-update) | async-done | bytes 1048592 | tf_op jit(solution)/shard_map/all_gather | solution.py:37
  52.8 40.5 %all-gather.5.cloned.1.call-done = bf16[2048,256]{0,1:T(8,128)(2,1)} async-done(((bf16[256,256]{0,1:T(8,128)(2,1)}), bf16[2048,256]{0,1:T(8,128)(2,1)}) %all-gather.5.cloned.1.call-update) | async-done | bytes 1048592 | tf_op jit(solution)/shard_map/all_gather | solution.py:38
  93.5 141.2 %while.27 = (s32[]{:T(128)}, f32[2,8,128]{2,1,0:T(8,128)S(1)}, f32[2,8,128]{2,1,0:T(8,128)S(1)}, f32[2,8,128,128]{3,2,1,0:T(8,128)S(1)}, f32[2,8,128]{2,1,0:T(8,...) while((s32[]{:T(128)}, f32[2,8,128]{2,1,0:T(8,128)S(1)}, ...), condition=%wide.region_10.11_spmd.clone.clone, body=%wide.region_1.10_spmd.clone.clone.sunk | while | flops 274260000 | bytes 12501754 | solution.py:86
  98.9 2.0 conditional.8
  106.3 3.3 %conditional.9 = ((f32[2,8,128]{2,1,0:T(8,128)S(1)}, f32[2,8,128]{2,1,0:T(8,128)S(1)}, f32[2,8,128,128]{3,2,1,0:T(8,128)S(1)})) conditional(s32[]{:T(128)} %bitcast.60, (f32[2,8,128]{2,1,0:T(8,128)S(1)}, f32[2,8,128]{2,1,0:T(8,128)S(1)}, f32[2,8,128,128]{3,2,1,0:T(8,128)S(1)}) %tuple.96, (s32[2]{0:T(128)S(1)}, s32[]{:T(128)}, ...), branch_computations={%region_6.6_spmd, %region_7.9_spmd} | conditional | flops 137121792 | bytes 6111282 | solution.py:77
  115.0 2.0 conditional.8
  117.1 3.3 %conditional.9 = ((f32[2,8,128]{2,1,0:T(8,128)S(1)}, f32[2,8,128]{2,1,0:T(8,128)S(1)}, f32[2,8,128,128]{3,2,1,0:T(8,128)S(1)})) conditional(s32[]{:T(128)} %bitcast.60, (f32[2,8,128]{2,1,0:T(8,128)S(1)}, f32[2,8,128]{2,1,0:T(8,128)S(1)}, f32[2,8,128,128]{3,2,1,0:T(8,128)S(1)}) %tuple.96, (s32[2]{0:T(128)S(1)}, s32[]{:T(128)}, ...), branch_computations={%region_6.6_spmd, %region_7.9_spmd} | conditional | flops 137121792 | bytes 6111282 | solution.py:77
  125.8 2.0 conditional.8
  127.8 3.3 %conditional.9 = ((f32[2,8,128]{2,1,0:T(8,128)S(1)}, f32[2,8,128]{2,1,0:T(8,128)S(1)}, f32[2,8,128,128]{3,2,1,0:T(8,128)S(1)})) conditional(s32[]{:T(128)} %bitcast.60, (f32[2,8,128]{2,1,0:T(8,128)S(1)}, f32[2,8,128]{2,1,0:T(8,128)S(1)}, f32[2,8,128,128]{3,2,1,0:T(8,128)S(1)}) %tuple.96, (s32[2]{0:T(128)S(1)}, s32[]{:T(128)}, ...), branch_computations={%region_6.6_spmd, %region_7.9_spmd} | conditional | flops 137121792 | bytes 6111282 | solution.py:77
  136.5 2.0 conditional.8
  138.5 3.3 %conditional.9 = ((f32[2,8,128]{2,1,0:T(8,128)S(1)}, f32[2,8,128]{2,1,0:T(8,128)S(1)}, f32[2,8,128,128]{3,2,1,0:T(8,128)S(1)})) conditional(s32[]{:T(128)} %bitcast.60, (f32[2,8,128]{2,1,0:T(8,128)S(1)}, f32[2,8,128]{2,1,0:T(8,128)S(1)}, f32[2,8,128,128]{3,2,1,0:T(8,128)S(1)}) %tuple.96, (s32[2]{0:T(128)S(1)}, s32[]{:T(128)}, ...), branch_computations={%region_6.6_spmd, %region_7.9_spmd} | conditional | flops 137121792 | bytes 6111282 | solution.py:77
  147.2 2.0 conditional.8
  149.2 3.3 %conditional.9 = ((f32[2,8,128]{2,1,0:T(8,128)S(1)}, f32[2,8,128]{2,1,0:T(8,128)S(1)}, f32[2,8,128,128]{3,2,1,0:T(8,128)S(1)})) conditional(s32[]{:T(128)} %bitcast.60, (f32[2,8,128]{2,1,0:T(8,128)S(1)}, f32[2,8,128]{2,1,0:T(8,128)S(1)}, f32[2,8,128,128]{3,2,1,0:T(8,128)S(1)}) %tuple.96, (s32[2]{0:T(128)S(1)}, s32[]{:T(128)}, ...), branch_computations={%region_6.6_spmd, %region_7.9_spmd} | conditional | flops 137121792 | bytes 6111282 | solution.py:77
  163.4 3.3 %conditional.9 = ((f32[2,8,128]{2,1,0:T(8,128)S(1)}, f32[2,8,128]{2,1,0:T(8,128)S(1)}, f32[2,8,128,128]{3,2,1,0:T(8,128)S(1)})) conditional(s32[]{:T(128)} %bitcast.60, (f32[2,8,128]{2,1,0:T(8,128)S(1)}, f32[2,8,128]{2,1,0:T(8,128)S(1)}, f32[2,8,128,128]{3,2,1,0:T(8,128)S(1)}) %tuple.96, (s32[2]{0:T(128)S(1)}, s32[]{:T(128)}, ...), branch_computations={%region_6.6_spmd, %region_7.9_spmd} | conditional | flops 137121792 | bytes 6111282 | solution.py:77
  172.1 3.3 %conditional.9 = ((f32[2,8,128]{2,1,0:T(8,128)S(1)}, f32[2,8,128]{2,1,0:T(8,128)S(1)}, f32[2,8,128,128]{3,2,1,0:T(8,128)S(1)})) conditional(s32[]{:T(128)} %bitcast.60, (f32[2,8,128]{2,1,0:T(8,128)S(1)}, f32[2,8,128]{2,1,0:T(8,128)S(1)}, f32[2,8,128,128]{3,2,1,0:T(8,128)S(1)}) %tuple.96, (s32[2]{0:T(128)S(1)}, s32[]{:T(128)}, ...), branch_computations={%region_6.6_spmd, %region_7.9_spmd} | conditional | flops 137121792 | bytes 6111282 | solution.py:77
  180.8 2.0 conditional.8
  182.8 3.3 %conditional.9 = ((f32[2,8,128]{2,1,0:T(8,128)S(1)}, f32[2,8,128]{2,1,0:T(8,128)S(1)}, f32[2,8,128,128]{3,2,1,0:T(8,128)S(1)})) conditional(s32[]{:T(128)} %bitcast.60, (f32[2,8,128]{2,1,0:T(8,128)S(1)}, f32[2,8,128]{2,1,0:T(8,128)S(1)}, f32[2,8,128,128]{3,2,1,0:T(8,128)S(1)}) %tuple.96, (s32[2]{0:T(128)S(1)}, s32[]{:T(128)}, ...), branch_computations={%region_6.6_spmd, %region_7.9_spmd} | conditional | flops 137121792 | bytes 6111282 | solution.py:77
  191.5 2.0 conditional.8
  193.5 3.3 %conditional.9 = ((f32[2,8,128]{2,1,0:T(8,128)S(1)}, f32[2,8,128]{2,1,0:T(8,128)S(1)}, f32[2,8,128,128]{3,2,1,0:T(8,128)S(1)})) conditional(s32[]{:T(128)} %bitcast.60, (f32[2,8,128]{2,1,0:T(8,128)S(1)}, f32[2,8,128]{2,1,0:T(8,128)S(1)}, f32[2,8,128,128]{3,2,1,0:T(8,128)S(1)}) %tuple.96, (s32[2]{0:T(128)S(1)}, s32[]{:T(128)}, ...), branch_computations={%region_6.6_spmd, %region_7.9_spmd} | conditional | flops 137121792 | bytes 6111282 | solution.py:77
  207.7 3.3 %conditional.9 = ((f32[2,8,128]{2,1,0:T(8,128)S(1)}, f32[2,8,128]{2,1,0:T(8,128)S(1)}, f32[2,8,128,128]{3,2,1,0:T(8,128)S(1)})) conditional(s32[]{:T(128)} %bitcast.60, (f32[2,8,128]{2,1,0:T(8,128)S(1)}, f32[2,8,128]{2,1,0:T(8,128)S(1)}, f32[2,8,128,128]{3,2,1,0:T(8,128)S(1)}) %tuple.96, (s32[2]{0:T(128)S(1)}, s32[]{:T(128)}, ...), branch_computations={%region_6.6_spmd, %region_7.9_spmd} | conditional | flops 137121792 | bytes 6111282 | solution.py:77
  221.9 2.0 conditional.8
  229.4 2.0 conditional.8
  231.4 3.3 %conditional.9 = ((f32[2,8,128]{2,1,0:T(8,128)S(1)}, f32[2,8,128]{2,1,0:T(8,128)S(1)}, f32[2,8,128,128]{3,2,1,0:T(8,128)S(1)})) conditional(s32[]{:T(128)} %bitcast.60, (f32[2,8,128]{2,1,0:T(8,128)S(1)}, f32[2,8,128]{2,1,0:T(8,128)S(1)}, f32[2,8,128,128]{3,2,1,0:T(8,128)S(1)}) %tuple.96, (s32[2]{0:T(128)S(1)}, s32[]{:T(128)}, ...), branch_computations={%region_6.6_spmd, %region_7.9_spmd} | conditional | flops 137121792 | bytes 6111282 | solution.py:77
  236.6 4.6 %all_to_all.16 = bf16[2,128,2048]{2,1,0:T(8,128)(2,1)S(1)} all-to-all(bf16[2,128,2048]{2,1,0:T(8,128)(2,1)S(1)} %convert_element_type.44), channel_id=1, replica_groups=mesh['rep'=2,'ctx'=8,'tp'=2] {'tp'}, dimensions={0} | all-to-all | bytes 2097152 | tf_op jit(solution)/shard_map/all_to_all | solution.py:97
  (258 shorter events, 78.4 us)
Async XLA Ops:
  7.2 5.8 %copy-start = (s32[16,12]{1,0:T(8,128)S(1)}, s32[16,12]{1,0:T(8,128)}, u32[]{:S(2)}) copy-start(s32[16,12]{1,0:T(8,128)} %param.15) | copy-start | bytes 2308
  7.2 45.6 %all-gather.3.cloned.1.call-start = ((), (), s32[]{:S(2)}) async-start(), calls=%async_computation.1 | async-start | bytes 1179648 | tf_op jit(solution)/shard_map/all_gather | solution.py:37
  8.9 84.3 %all-gather.5.cloned.1.call-start = ((), (), s32[]{:S(2)}) async-start(), calls=%async_computation.2 | async-start | bytes 1179648 | tf_op jit(solution)/shard_map/all_gather | solution.py:38
  12.1 0.7 copy-start.1
Sparse Core Ops, SparseCore 0:
  10.6 42.1 all-gather.2
  54.8 38.3 all-gather.4
where the time goes:
time: 253 us; the launch traced here: 251 us
  waiting for transfers between devices  79.6 us (31%)
  loops' own time  74.1 us (29%)
  local copies, waits for them, and re-layouts  50.8 us (20%)
  matrix products  21 us (8%)
  between operations  14.2 us (6%)
  other arithmetic  6.35 us (3%)
  blocking collectives  4.58 us (2%)
    another operation x1, loops' own time, body(): states = lax.fori_loop(0, key_blocks, one_key_block, carried)  52.4 us
    all_gather x1, waiting for transfers between devices, body(): value_piece = lax.all_gather(ordered_value_rows, 'ctx', axis=0, tiled=True)  40.5 us
    all_gather x1, waiting for transfers between devices, body(): key_piece = lax.all_gather(rotated_key_rows, 'ctx', axis=0, tiled=True)  39.1 us
    another operation x32, loops' own time, one_key_block(): lax.cond(live_table[block_local, key_seq], compute_tile, lambda current:...  21.7 us
    dynamic_slice x16, local copies, waits for them, and re-layouts, one_key_block(): lax.dynamic_slice_in_dim(value_piece, offset, BLOCK_TOKENS)  14.3 us
    dot_general x20, matrix products, compute_tile(): jnp.einsum('hgqk,khd->hgqd', weights.astype(jnp.bfloat16), value_part, pr...  13.7 us
    dynamic_slice x16, local copies, waits for them, and re-layouts, one_key_block(): live_table[block_local, key_seq]  10.6 us
    dynamic_slice x16, local copies, waits for them, and re-layouts, one_key_block(): key_seq = block_order[offset // BLOCK_TOKENS]  9.39 us
  transfers between devices with their start and end apart: 2, of which 2 were waited for; matrix products, arithmetic and copies ran while one was open for 2% of the time, Pallas kernels for 0%

commit v1 on v0

--- a/solution.py
+++ b/solution.py
@@ -35,7 +35,21 @@
         )
     )
     key_piece = lax.all_gather(rotated_key_rows, "ctx", axis=0, tiled=True)
-    value_piece = lax.all_gather(ordered_value_rows, "ctx", axis=0, tiled=True)
+    ways, here, step = (lax.axis_size("ctx"), lax.axis_index("ctx"), ordered_value_rows.shape[0])
+    dims = [n * ways if d == 0 else n for d, n in enumerate(ordered_value_rows.shape)]
+    full = lax.dynamic_update_slice_in_dim(
+        jnp.zeros(dims, ordered_value_rows.dtype), ordered_value_rows, here * step, axis=0
+    )
+    going_up = going_down = ordered_value_rows
+    for far in range(1, ways // 2 + 1):
+        going_up = lax.ppermute(going_up, "ctx", [(d, (d + 1) % ways) for d in range(ways)])
+        full = lax.dynamic_update_slice_in_dim(full, going_up, (here - far) % ways * step, axis=0)
+        if 2 * far < ways:
+            going_down = lax.ppermute(going_down, "ctx", [(d, (d - 1) % ways) for d in range(ways)])
+            full = lax.dynamic_update_slice_in_dim(
+                full, going_down, (here + far) % ways * step, axis=0
+            )
+    value_piece = full
     key_blocks = key_piece.shape[0] // BLOCK_TOKENS
 
     def one_key_block(turn_index, states):

time: 253 us -> 211 us (0.83)
  waiting for transfers between devices: 79.6 us -> 21.8 us
  starting transfers between devices: 0.08 us -> 16.2 us
  loops' own time: 74.1 us -> 68 us
  local copies, waits for them, and re-layouts: 50.8 us -> 56.2 us
    all_gather x1 -> x0, waiting for transfers between devices: 40.5 us -> none  [body(): value_piece = lax.all_gather(ordered_value_rows, 'ctx', axis=0, tiled=True)]
    all_gather x1, waiting for transfers between devices: 39.1 us -> 4.22 us  [body(): key_piece = lax.all_gather(rotated_key_rows, 'ctx', axis=0, tiled=True)]
    ppermute x0 -> x7, waiting for transfers between devices: none -> 17.6 us  [the longest x4 15.3 us: body(): lax.ppermute(going_up, 'ctx', [(d, (d + 1) % ways) for d in range(ways)])]
    ppermute x0 -> x7, starting transfers between devices: none -> 16.2 us  [the longest x3 16.2 us: body(): lax.ppermute(going_down, 'ctx', [(d, (d - 1) % ways) for d in range(ways)])]
    dynamic_update_slice x0 -> x8, local copies, waits for them, and re-layouts: none -> 5.31 us  [the longest x4 2.66 us: body(): lax.dynamic_update_slice_in_dim(full, going_up, (here - far) % ways * ste...]
    another operation x1, loops' own time: 52.4 us -> 48.6 us  [body(): states = lax.fori_loop(0, key_blocks, one_key_block, carried)]
  transfers between devices with their start and end apart: 2 -> 8, of which waited for: 2 -> 4; matrix products, arithmetic and copies ran while one was open for 2% -> 5% of each run, Pallas kernels for 0% -> 0%
where the time goes in v1:
time: 211 us; the launch traced here: 209 us
  loops' own time  68 us (32%)
  local copies, waits for them, and re-layouts  56.2 us (27%)
  waiting for transfers between devices  21.8 us (10%)
  matrix products  21 us (10%)
  starting transfers between devices  16.2 us (8%)
  between operations  14.3 us (7%)
  other arithmetic  6.99 us (3%)
  blocking collectives  4.58 us (2%)
    another operation x1, loops' own time, body(): states = lax.fori_loop(0, key_blocks, one_key_block, carried)  48.6 us
    another operation x32, loops' own time, one_key_block(): lax.cond(live_table[block_local, key_seq], compute_tile, lambda current:...  19.3 us
    ppermute x3, starting transfers between devices, body(): lax.ppermute(going_down, 'ctx', [(d, (d - 1) % ways) for d in range(ways)])  16.2 us
    ppermute x4, waiting for transfers between devices, body(): lax.ppermute(going_up, 'ctx', [(d, (d + 1) % ways) for d in range(ways)])  15.3 us
    dynamic_slice x16, local copies, waits for them, and re-layouts, one_key_block(): lax.dynamic_slice_in_dim(value_piece, offset, BLOCK_TOKENS)  14.2 us
    dot_general x20, matrix products, compute_tile(): jnp.einsum('hgqk,khd->hgqd', weights.astype(jnp.bfloat16), value_part, pr...  13.7 us
    dynamic_slice x16, local copies, waits for them, and re-layouts, one_key_block(): live_table[block_local, key_seq]  10.8 us
    dynamic_slice x16, local copies, waits for them, and re-layouts, one_key_block(): key_seq = block_order[offset // BLOCK_TOKENS]  9.25 us
  transfers between devices with their start and end apart: 8, of which 4 were waited for; matrix products, arithmetic and copies ran while one was open for 5% of the time, Pallas kernels for 0%

profile of v1, /device:TPU:0, one launch (start us, length us, event | category | flops | bytes accessed | tf_op | source)
XLA Modules:
  0.0 209.1 jit_solution(9342380660541550558)
XLA Ops:
  9.9 6.1 %collective-permute-start.1 = (bf16[256,256]{0,1:T(8,128)(2,1)S(1)}, bf16[256,256]{0,1:T(8,128)(2,1)S(1)}, u32[]{:S(2)}, u32[]{:S(2)}) collective-permute-start(bf16[256,256]{0,1:T(8,128)(2,1)S(1)} %copy.44), channel_id=1, source_target_pairs={{0,14},{2,0},{4,2},{6,4},{8,6},{10,8},{12,10},{14,12},{1,15},{3,1}... | collective-permute-start | bytes 393224 | tf_op jit(solution)/shard_map/ppermute | solution.py:48
  21.6 4.7 %collective-permute-start.3 = (bf16[256,256]{0,1:T(8,128)(2,1)S(1)}, bf16[256,256]{0,1:T(8,128)(2,1)S(1)}, u32[]{:S(2)}, u32[]{:S(2)}) collective-permute-start(bf16[256,256]{0,1:T(8,128)(2,1)S(1)} %collective-permute-done.1), channel_id=1, source_target_pairs={{0,14},{2,0},{4,2},{6,4},{8,6},{10,8},{12,10},{14,12},{1,15},{3,1}... | collective-permute-start | bytes 393224 | tf_op jit(solution)/shard_map/ppermute | solution.py:48
  27.6 2.3 %collective-permute-done.3 = bf16[256,256]{0,1:T(8,128)(2,1)S(1)} collective-permute-done((bf16[256,256]{0,1:T(8,128)(2,1)S(1)}, bf16[256,256]{0,1:T(8,128)(2,1)S(1)}, u32[]{:S(2)}, u32[]{:S(2)}) %collective-permute-start.3) | collective-permute-done | bytes 131104 | tf_op jit(solution)/shard_map/ppermute | solution.py:48
  29.9 5.4 %collective-permute-start.5 = (bf16[256,256]{0,1:T(8,128)(2,1)S(1)}, bf16[256,256]{0,1:T(8,128)(2,1)S(1)}, u32[]{:S(2)}, u32[]{:S(2)}) collective-permute-start(bf16[256,256]{0,1:T(8,128)(2,1)S(1)} %collective-permute-done.3), channel_id=1, source_target_pairs={{0,14},{2,0},{4,2},{6,4},{8,6},{10,8},{12,10},{14,12},{1,15},{3,1}... | collective-permute-start | bytes 393224 | tf_op jit(solution)/shard_map/ppermute | solution.py:48
  36.6 6.3 %collective-permute-done.4 = bf16[256,256]{0,1:T(8,128)(2,1)S(1)} collective-permute-done((bf16[256,256]{0,1:T(8,128)(2,1)S(1)}, bf16[256,256]{0,1:T(8,128)(2,1)S(1)}, u32[]{:S(2)}, u32[]{:S(2)}) %collective-permute-start.4) | collective-permute-done | bytes 131104 | tf_op jit(solution)/shard_map/ppermute | solution.py:45
  44.3 9.0 %collective-permute-done.6 = bf16[256,256]{0,1:T(8,128)(2,1)S(1)} collective-permute-done((bf16[256,256]{0,1:T(8,128)(2,1)S(1)}, bf16[256,256]{0,1:T(8,128)(2,1)S(1)}, u32[]{:S(2)}, u32[]{:S(2)}) %collective-permute-start.6) | collective-permute-done | bytes 131104 | tf_op jit(solution)/shard_map/ppermute | solution.py:45
  53.9 4.2 %all-gather.2.cloned.1.call-done = bf16[2048,256]{0,1:T(8,128)(2,1)} async-done(((bf16[256,256]{0,1:T(8,128)(2,1)}), bf16[2048,256]{0,1:T(8,128)(2,1)}) %all-gather.2.cloned.1.call-update) | async-done | bytes 1048592 | tf_op jit(solution)/shard_map/all_gather | solution.py:37
  58.8 134.3 %while.27 = (s32[]{:T(128)}, f32[2,8,128]{2,1,0:T(8,128)S(1)}, f32[2,8,128]{2,1,0:T(8,128)S(1)}, f32[2,8,128,128]{3,2,1,0:T(8,128)S(1)}, f32[2,8,128]{2,1,0:T(8,...) while((s32[]{:T(128)}, f32[2,8,128]{2,1,0:T(8,128)S(1)}, ...), condition=%wide.region_10.11_spmd.clone.clone, body=%wide.region_1.10_spmd.clone.clone.sunk | while | flops 274260000 | bytes 12501754 | solution.py:100
  63.9 1.9 conditional.8
  71.1 3.1 %conditional.9 = ((f32[2,8,128]{2,1,0:T(8,128)S(1)}, f32[2,8,128]{2,1,0:T(8,128)S(1)}, f32[2,8,128,128]{3,2,1,0:T(8,128)S(1)})) conditional(s32[]{:T(128)} %bitcast.60, (f32[2,8,128]{2,1,0:T(8,128)S(1)}, f32[2,8,128]{2,1,0:T(8,128)S(1)}, f32[2,8,128,128]{3,2,1,0:T(8,128)S(1)}) %tuple.96, (s32[2]{0:T(128)S(1)}, s32[]{:T(128)}, ...), branch_computations={%region_6.6_spmd, %region_7.9_spmd} | conditional | flops 137121792 | bytes 6111282 | solution.py:91
  81.3 3.1 %conditional.9 = ((f32[2,8,128]{2,1,0:T(8,128)S(1)}, f32[2,8,128]{2,1,0:T(8,128)S(1)}, f32[2,8,128,128]{3,2,1,0:T(8,128)S(1)})) conditional(s32[]{:T(128)} %bitcast.60, (f32[2,8,128]{2,1,0:T(8,128)S(1)}, f32[2,8,128]{2,1,0:T(8,128)S(1)}, f32[2,8,128,128]{3,2,1,0:T(8,128)S(1)}) %tuple.96, (s32[2]{0:T(128)S(1)}, s32[]{:T(128)}, ...), branch_computations={%region_6.6_spmd, %region_7.9_spmd} | conditional | flops 137121792 | bytes 6111282 | solution.py:91
  91.4 3.1 %conditional.9 = ((f32[2,8,128]{2,1,0:T(8,128)S(1)}, f32[2,8,128]{2,1,0:T(8,128)S(1)}, f32[2,8,128,128]{3,2,1,0:T(8,128)S(1)})) conditional(s32[]{:T(128)} %bitcast.60, (f32[2,8,128]{2,1,0:T(8,128)S(1)}, f32[2,8,128]{2,1,0:T(8,128)S(1)}, f32[2,8,128,128]{3,2,1,0:T(8,128)S(1)}) %tuple.96, (s32[2]{0:T(128)S(1)}, s32[]{:T(128)}, ...), branch_computations={%region_6.6_spmd, %region_7.9_spmd} | conditional | flops 137121792 | bytes 6111282 | solution.py:91
  99.7 1.9 conditional.8
  101.6 3.1 %conditional.9 = ((f32[2,8,128]{2,1,0:T(8,128)S(1)}, f32[2,8,128]{2,1,0:T(8,128)S(1)}, f32[2,8,128,128]{3,2,1,0:T(8,128)S(1)})) conditional(s32[]{:T(128)} %bitcast.60, (f32[2,8,128]{2,1,0:T(8,128)S(1)}, f32[2,8,128]{2,1,0:T(8,128)S(1)}, f32[2,8,128,128]{3,2,1,0:T(8,128)S(1)}) %tuple.96, (s32[2]{0:T(128)S(1)}, s32[]{:T(128)}, ...), branch_computations={%region_6.6_spmd, %region_7.9_spmd} | conditional | flops 137121792 | bytes 6111282 | solution.py:91
  109.9 1.9 conditional.8
  111.8 3.1 %conditional.9 = ((f32[2,8,128]{2,1,0:T(8,128)S(1)}, f32[2,8,128]{2,1,0:T(8,128)S(1)}, f32[2,8,128,128]{3,2,1,0:T(8,128)S(1)})) conditional(s32[]{:T(128)} %bitcast.60, (f32[2,8,128]{2,1,0:T(8,128)S(1)}, f32[2,8,128]{2,1,0:T(8,128)S(1)}, f32[2,8,128,128]{3,2,1,0:T(8,128)S(1)}) %tuple.96, (s32[2]{0:T(128)S(1)}, s32[]{:T(128)}, ...), branch_computations={%region_6.6_spmd, %region_7.9_spmd} | conditional | flops 137121792 | bytes 6111282 | solution.py:91
  125.3 3.1 %conditional.9 = ((f32[2,8,128]{2,1,0:T(8,128)S(1)}, f32[2,8,128]{2,1,0:T(8,128)S(1)}, f32[2,8,128,128]{3,2,1,0:T(8,128)S(1)})) conditional(s32[]{:T(128)} %bitcast.60, (f32[2,8,128]{2,1,0:T(8,128)S(1)}, f32[2,8,128]{2,1,0:T(8,128)S(1)}, f32[2,8,128,128]{3,2,1,0:T(8,128)S(1)}) %tuple.96, (s32[2]{0:T(128)S(1)}, s32[]{:T(128)}, ...), branch_computations={%region_6.6_spmd, %region_7.9_spmd} | conditional | flops 137121792 | bytes 6111282 | solution.py:91
  133.6 3.1 %conditional.9 = ((f32[2,8,128]{2,1,0:T(8,128)S(1)}, f32[2,8,128]{2,1,0:T(8,128)S(1)}, f32[2,8,128,128]{3,2,1,0:T(8,128)S(1)})) conditional(s32[]{:T(128)} %bitcast.60, (f32[2,8,128]{2,1,0:T(8,128)S(1)}, f32[2,8,128]{2,1,0:T(8,128)S(1)}, f32[2,8,128,128]{3,2,1,0:T(8,128)S(1)}) %tuple.96, (s32[2]{0:T(128)S(1)}, s32[]{:T(128)}, ...), branch_computations={%region_6.6_spmd, %region_7.9_spmd} | conditional | flops 137121792 | bytes 6111282 | solution.py:91
  143.8 3.1 %conditional.9 = ((f32[2,8,128]{2,1,0:T(8,128)S(1)}, f32[2,8,128]{2,1,0:T(8,128)S(1)}, f32[2,8,128,128]{3,2,1,0:T(8,128)S(1)})) conditional(s32[]{:T(128)} %bitcast.60, (f32[2,8,128]{2,1,0:T(8,128)S(1)}, f32[2,8,128]{2,1,0:T(8,128)S(1)}, f32[2,8,128,128]{3,2,1,0:T(8,128)S(1)}) %tuple.96, (s32[2]{0:T(128)S(1)}, s32[]{:T(128)}, ...), branch_computations={%region_6.6_spmd, %region_7.9_spmd} | conditional | flops 137121792 | bytes 6111282 | solution.py:91
  152.0 1.9 conditional.8
  154.0 3.1 %conditional.9 = ((f32[2,8,128]{2,1,0:T(8,128)S(1)}, f32[2,8,128]{2,1,0:T(8,128)S(1)}, f32[2,8,128,128]{3,2,1,0:T(8,128)S(1)})) conditional(s32[]{:T(128)} %bitcast.60, (f32[2,8,128]{2,1,0:T(8,128)S(1)}, f32[2,8,128]{2,1,0:T(8,128)S(1)}, f32[2,8,128,128]{3,2,1,0:T(8,128)S(1)}) %tuple.96, (s32[2]{0:T(128)S(1)}, s32[]{:T(128)}, ...), branch_computations={%region_6.6_spmd, %region_7.9_spmd} | conditional | flops 137121792 | bytes 6111282 | solution.py:91
  167.5 3.1 %conditional.9 = ((f32[2,8,128]{2,1,0:T(8,128)S(1)}, f32[2,8,128]{2,1,0:T(8,128)S(1)}, f32[2,8,128,128]{3,2,1,0:T(8,128)S(1)})) conditional(s32[]{:T(128)} %bitcast.60, (f32[2,8,128]{2,1,0:T(8,128)S(1)}, f32[2,8,128]{2,1,0:T(8,128)S(1)}, f32[2,8,128,128]{3,2,1,0:T(8,128)S(1)}) %tuple.96, (s32[2]{0:T(128)S(1)}, s32[]{:T(128)}, ...), branch_computations={%region_6.6_spmd, %region_7.9_spmd} | conditional | flops 137121792 | bytes 6111282 | solution.py:91
  190.0 3.1 %conditional.9 = ((f32[2,8,128]{2,1,0:T(8,128)S(1)}, f32[2,8,128]{2,1,0:T(8,128)S(1)}, f32[2,8,128,128]{3,2,1,0:T(8,128)S(1)})) conditional(s32[]{:T(128)} %bitcast.60, (f32[2,8,128]{2,1,0:T(8,128)S(1)}, f32[2,8,128]{2,1,0:T(8,128)S(1)}, f32[2,8,128,128]{3,2,1,0:T(8,128)S(1)}) %tuple.96, (s32[2]{0:T(128)S(1)}, s32[]{:T(128)}, ...), branch_computations={%region_6.6_spmd, %region_7.9_spmd} | conditional | flops 137121792 | bytes 6111282 | solution.py:91
  195.1 4.6 %all_to_all.16 = bf16[2,128,2048]{2,1,0:T(8,128)(2,1)S(1)} all-to-all(bf16[2,128,2048]{2,1,0:T(8,128)(2,1)S(1)} %convert_element_type.44), channel_id=1, replica_groups=mesh['rep'=2,'ctx'=8,'tp'=2] {'tp'}, dimensions={0} | all-to-all | bytes 2097152 | tf_op jit(solution)/shard_map/all_to_all | solution.py:111
  (278 shorter events, 94.0 us)
Async XLA Ops:
  7.2 9.6 %copy-start = (s32[16,12]{1,0:T(8,128)S(1)}, s32[16,12]{1,0:T(8,128)}, u32[]{:S(2)}) copy-start(s32[16,12]{1,0:T(8,128)} %param.15) | copy-start | bytes 2308
  7.2 51.0 %all-gather.2.cloned.1.call-start = ((), (), s32[]{:S(2)}) async-start(), calls=%async_computation.1 | async-start | bytes 1179648 | tf_op jit(solution)/shard_map/all_gather | solution.py:37
  9.9 11.7 %collective-permute-start.1 = (bf16[256,256]{0,1:T(8,128)(2,1)S(1)}, bf16[256,256]{0,1:T(8,128)(2,1)S(1)}, u32[]{:S(2)}, u32[]{:S(2)}) collective-permute-start(bf16[256,256]{0,1:T(8,128)(2,1)S(1)} %copy.44), channel_id=1, source_target_pairs={{0,14},{2,0},{4,2},{6,4},{8,6},{10,8},{12,10},{14,12},{1,15},{3,1}... | collective-permute-start | bytes 393224 | tf_op jit(solution)/shard_map/ppermute | solution.py:48
  16.0 10.3 %collective-permute-start = (bf16[256,256]{0,1:T(8,128)(2,1)S(1)}, bf16[256,256]{0,1:T(8,128)(2,1)S(1)}, u32[]{:S(2)}, u32[]{:S(2)}) collective-permute-start(bf16[256,256]{0,1:T(8,128)(2,1)S(1)} %copy.44), channel_id=1, source_target_pairs={{0,2},{2,4},{4,6},{6,8},{8,10},{10,12},{12,14},{14,0},{1,3},{3,5},... | collective-permute-start | bytes 393224 | tf_op jit(solution)/shard_map/ppermute | solution.py:45
  21.6 8.3 %collective-permute-start.3 = (bf16[256,256]{0,1:T(8,128)(2,1)S(1)}, bf16[256,256]{0,1:T(8,128)(2,1)S(1)}, u32[]{:S(2)}, u32[]{:S(2)}) collective-permute-start(bf16[256,256]{0,1:T(8,128)(2,1)S(1)} %collective-permute-done.1), channel_id=1, source_target_pairs={{0,14},{2,0},{4,2},{6,4},{8,6},{10,8},{12,10},{14,12},{1,15},{3,1}... | collective-permute-start | bytes 393224 | tf_op jit(solution)/shard_map/ppermute | solution.py:48
  26.3 9.0 %collective-permute-start.2 = (bf16[256,256]{0,1:T(8,128)(2,1)S(1)}, bf16[256,256]{0,1:T(8,128)(2,1)S(1)}, u32[]{:S(2)}, u32[]{:S(2)}) collective-permute-start(bf16[256,256]{0,1:T(8,128)(2,1)S(1)} %collective-permute-done), channel_id=1, source_target_pairs={{0,2},{2,4},{4,6},{6,8},{8,10},{10,12},{12,14},{14,0},{1,3},{3,5},... | collective-permute-start | bytes 393224 | tf_op jit(solution)/shard_map/ppermute | solution.py:45
  29.9 13.7 %collective-permute-start.5 = (bf16[256,256]{0,1:T(8,128)(2,1)S(1)}, bf16[256,256]{0,1:T(8,128)(2,1)S(1)}, u32[]{:S(2)}, u32[]{:S(2)}) collective-permute-start(bf16[256,256]{0,1:T(8,128)(2,1)S(1)} %collective-permute-done.3), channel_id=1, source_target_pairs={{0,14},{2,0},{4,2},{6,4},{8,6},{10,8},{12,10},{14,12},{1,15},{3,1}... | collective-permute-start | bytes 393224 | tf_op jit(solution)/shard_map/ppermute | solution.py:48
  35.3 7.7 %collective-permute-start.4 = (bf16[256,256]{0,1:T(8,128)(2,1)S(1)}, bf16[256,256]{0,1:T(8,128)(2,1)S(1)}, u32[]{:S(2)}, u32[]{:S(2)}) collective-permute-start(bf16[256,256]{0,1:T(8,128)(2,1)S(1)} %collective-permute-done.2), channel_id=1, source_target_pairs={{0,2},{2,4},{4,6},{6,8},{8,10},{10,12},{12,14},{14,0},{1,3},{3,5},... | collective-permute-start | bytes 393224 | tf_op jit(solution)/shard_map/ppermute | solution.py:45
  42.9 10.3 %collective-permute-start.6 = (bf16[256,256]{0,1:T(8,128)(2,1)S(1)}, bf16[256,256]{0,1:T(8,128)(2,1)S(1)}, u32[]{:S(2)}, u32[]{:S(2)}) collective-permute-start(bf16[256,256]{0,1:T(8,128)(2,1)S(1)} %collective-permute-done.4), channel_id=1, source_target_pairs={{0,2},{2,4},{4,6},{6,8},{8,10},{10,12},{12,14},{14,0},{1,3},{3,5},... | collective-permute-start | bytes 393224 | tf_op jit(solution)/shard_map/ppermute | solution.py:45
  58.1 0.7 copy-start.1
Sparse Core Ops, SparseCore 0:
  10.0 48.0 all-gather.1
